TPU v7x, 32 devices: a whole 2x2x4 slice. The times are simulated.
32 devices in a mesh: dp: 16 (over z, y, core), tensor: 2 (over x).
Axes of the slice: x: 2, y: 2, z: 4, core: 2. Of those that a mesh axis runs over, the one named last changes fastest.
Arguments:
- tokens: float32 [16384, 1024], P(('dp', 'tensor')), may hold values from -6 to 6
- norm_gain: float32 [1024], P(('dp', 'tensor')), may hold values from 0.5 to 1.5
- w_z: bfloat16 [1024, 2048], P('dp', 'tensor'), may hold values from -0.1875 to 0.1875
- w_x: bfloat16 [1024, 2048], P('dp', 'tensor'), may hold values from -0.1875 to 0.1875
- w_dt: bfloat16 [1024, 32], P('dp', 'tensor'), may hold values from -0.1875 to 0.1875
- w_bc: bfloat16 [1024, 256], P(('dp', 'tensor')), may hold values from -0.1875 to 0.1875
- w_out: bfloat16 [1024, 2048], P('dp', 'tensor'), may hold values from -0.125 to 0.125
- conv_x_w: float32 [2048, 4], P('tensor'), may hold values from -3 to 3
- conv_x_b: float32 [2048], P('tensor'), may hold values from -0.5 to 0.5
- conv_bc_w: float32 [256, 4], P(('dp', 'tensor')), may hold values from -3 to 3
- conv_bc_b: float32 [256], P(('dp', 'tensor')), may hold values from -0.5 to 0.5
- a_log: float32 [32], P('tensor'), may hold values from -1 to 1.5
- d_skip: float32 [32], P('tensor'), may hold values from 0.5 to 1.5
- dt_bias: float32 [32], P('tensor'), may hold values from -7 to -2.5
- norm_w: float32 [2048], P('tensor'), may hold values from 0.5 to 1.5
- block_seq: int32 [64], P('dp'), may hold values from 0 to 63, as said below
- block_len: int32 [64], P('dp'), may hold values from 0 to 256, as said below
- cotangent: float32 [16384, 1024], P(('dp', 'tensor')), may hold values from -6 to 6
Outputs:
- output: float32 [16384, 1024], P(('dp', 'tensor'))
- d_tokens: float32 [16384, 1024], P(('dp', 'tensor'))
- d_gain: float32 [1024], P(('dp', 'tensor'))
- d_w_z: float32 [1024, 2048], P('dp', 'tensor')
- d_w_x: float32 [1024, 2048], P('dp', 'tensor')
- d_w_dt: float32 [1024, 32], P('dp', 'tensor')
- d_w_bc: float32 [1024, 256], P(('dp', 'tensor'))
- d_w_out: float32 [1024, 2048], P('dp', 'tensor')
- d_conv_x_w: float32 [2048, 4], P('tensor')
- d_conv_x_b: float32 [2048], P('tensor')
- d_conv_bc_w: float32 [256, 4], P(('dp', 'tensor'))
- d_conv_bc_b: float32 [256], P(('dp', 'tensor'))
- d_a_log: float32 [32], P('tensor')
- d_d_skip: float32 [32], P('tensor')
- d_dt_bias: float32 [32], P('tensor')
- d_norm_w: float32 [2048], P('tensor')
Inputs may be any that keep to these rules, and one draw needn't show every extreme that they name: `block_seq`: each index of dp holds 4 slots; a sequence takes consecutive slots of one index starting at a slot's first row, every slot but its last full; adjacent slots of one index carry the same value exactly when they hold one sequence; an empty slot has a value no other slot has. `block_len`: rows in use count from a slot's start; an empty slot has 0; fewer than 256 only in a sequence's last slot.
All inputs are finite; a program needn't handle non-finite values.
Results may differ from a plain program's by a relative error of at most 0.0082.
Values may be sent and summed in bfloat16 or wider, within the bound.
A program may use at most 192 MiB of HBM per device.

v0:
```python
import jax
import jax.numpy as jnp
from jax import lax
from jax.sharding import PartitionSpec as P

INNER = 2048
HEADDIM = 64
STATE = 128
BLOCK = 256
EPSILON = 1e-05
HIGHEST_PREC = lax.Precision.HIGHEST


def shift_rows(values, lag_rows):
    if lag_rows == 0:
        return values
    zero_rows = jnp.zeros((lag_rows,) + values.shape[1:], values.dtype)
    return jnp.concatenate([zero_rows, values[:-lag_rows]], axis=0)


def causal_conv(values, weights, bias_vec, keep_masks):
    taps_count = weights.shape[1]
    summed = jnp.zeros_like(values) + bias_vec[None, :]
    for offset in range(taps_count):
        lag_rows = taps_count - 1 - offset
        shifted = shift_rows(values, lag_rows) * keep_masks[lag_rows][:, None]
        summed = summed + shifted * weights[:, offset][None, :]
    return jax.nn.silu(summed)


def scan_heads(
    x_pre,
    bc_pre,
    dt_raw,
    conv_x_w,
    conv_x_b,
    conv_bc_w,
    conv_bc_b,
    a_log,
    d_skip,
    dt_bias,
    carry_flags,
    token_mask,
):
    row_count = x_pre.shape[0]
    slot_count = row_count // BLOCK
    head_count = dt_raw.shape[1]
    position = jnp.arange(row_count) % BLOCK
    carry_rows = jnp.repeat(carry_flags, BLOCK)
    keep_masks = [
        jnp.where(position >= lag_rows, jnp.ones_like(carry_rows), carry_rows)
        for lag_rows in range(conv_x_w.shape[1])
    ]
    x_conv = causal_conv(x_pre, conv_x_w, conv_x_b, keep_masks)
    bc_conv = causal_conv(bc_pre, conv_bc_w, conv_bc_b, keep_masks)
    state_in = bc_conv[:, :STATE].reshape(slot_count, BLOCK, STATE)
    state_out = bc_conv[:, STATE:].reshape(slot_count, BLOCK, STATE)
    inputs = x_conv.reshape(slot_count, BLOCK, head_count, HEADDIM)
    steps_dt = jax.nn.softplus(dt_raw + dt_bias[None, :]) * token_mask[:, None]
    decay_rates = (steps_dt * (-jnp.exp(a_log))[None, :]).reshape(slot_count, BLOCK, head_count)
    steps_three = steps_dt.reshape(slot_count, BLOCK, head_count)
    lower_mask = (jnp.arange(BLOCK)[:, None] >= jnp.arange(BLOCK)[None, :]).astype(x_pre.dtype)
    cumulative = jnp.einsum("ij,sjh->sih", lower_mask, decay_rates, precision=HIGHEST_PREC)
    scores_cb = jnp.einsum("sin,sjn->sij", state_out, state_in, precision=HIGHEST_PREC)
    differ = cumulative[:, :, None, :] - cumulative[:, None, :, :]
    decay_mat = jnp.exp(jnp.where(lower_mask[None, :, :, None] > 0.5, differ, -1e30))
    mixing = scores_cb[:, :, :, None] * decay_mat * steps_three[:, None, :, :]
    y_local = jnp.einsum("sijh,sjhp->sihp", mixing, inputs, precision=HIGHEST_PREC)
    span_total = cumulative[:, -1, :]
    to_end = jnp.exp(span_total[:, None, :] - cumulative) * steps_three
    block_states = jnp.einsum(
        "sjn,sjh,sjhp->shnp", state_in, to_end, inputs, precision=HIGHEST_PREC
    )
    carried = []
    current = jnp.zeros((head_count, STATE, HEADDIM), x_pre.dtype)
    for slot_index in range(slot_count):
        current = current * carry_flags[slot_index]
        carried.append(current)
        current = (
            current * jnp.exp(span_total[slot_index])[:, None, None] + block_states[slot_index]
        )
    entering = jnp.stack(carried)
    y_state = (
        jnp.einsum("sin,shnp->sihp", state_out, entering, precision=HIGHEST_PREC)
        * jnp.exp(cumulative)[:, :, :, None]
    )
    output = y_local + y_state + inputs * d_skip[None, None, :, None]
    return output.reshape(row_count, head_count * HEADDIM)


def dot_nt(left, right):
    return lax.dot_general(
        left, right, (((1,), (1,)), ((), ())), preferred_element_type=jnp.float32
    )


def dot_tn(left, right):
    return lax.dot_general(
        left, right, (((0,), (0,)), ((), ())), preferred_element_type=jnp.float32
    )


def per_device(
    tokens,
    norm_gain,
    w_z,
    w_x,
    w_dt,
    w_bc,
    w_out,
    conv_x_w,
    conv_x_b,
    conv_bc_w,
    conv_bc_b,
    a_log,
    d_skip,
    dt_bias,
    norm_w,
    block_seq,
    block_len,
    cotangent,
):
    bc_full, gain_full, conv_bcw_full, conv_bcb_full = (
        lax.all_gather(w_bc.astype(jnp.float32), ("dp", "tensor"), axis=0, tiled=True),
        lax.all_gather(norm_gain, ("dp", "tensor"), axis=0, tiled=True),
        lax.all_gather(conv_bc_w, ("dp", "tensor"), axis=0, tiled=True),
        lax.all_gather(conv_bc_b, ("dp", "tensor"), axis=0, tiled=True),
    )
    bc_weight = bc_full.astype(jnp.bfloat16)
    mean_sq = jnp.mean(tokens * tokens, axis=1, keepdims=True)
    inv_rms = lax.rsqrt(mean_sq + EPSILON)
    unit_rows = tokens * inv_rms
    normed_own = (unit_rows * gain_full[None, :]).astype(jnp.bfloat16)
    normed = lax.all_gather(normed_own, "tensor", axis=0, tiled=True)
    z_full, x_full, dt_full, out_full = (
        lax.all_gather(w_z, "dp", axis=0, tiled=True),
        lax.all_gather(w_x, "dp", axis=0, tiled=True),
        lax.all_gather(w_dt, "dp", axis=0, tiled=True),
        lax.all_gather(w_out, "dp", axis=0, tiled=True),
    )
    row_count = normed.shape[0]
    slot_count = block_seq.shape[0]
    slot_index = jnp.arange(slot_count)
    previous = jnp.concatenate([block_seq[:1] - 1, block_seq[:-1]])
    carry_flags = ((slot_index > 0) & (block_seq == previous)).astype(jnp.float32)
    token_mask = (jnp.arange(row_count) % BLOCK < jnp.repeat(block_len, BLOCK)).astype(jnp.float32)
    gate_pre = jnp.dot(normed, z_full, preferred_element_type=jnp.float32)
    x_pre = jnp.dot(normed, x_full, preferred_element_type=jnp.float32)
    bc_pre = jnp.dot(normed, bc_weight, preferred_element_type=jnp.float32)
    dt_raw = jnp.dot(normed, dt_full, preferred_element_type=jnp.float32)

    def local_scan(xp_in, bc_in, dt_in, cxw, cxb, cbw, cbb, alog_in, skip_in, bias_in):
        return scan_heads(
            xp_in,
            bc_in,
            dt_in,
            cxw,
            cxb,
            cbw,
            cbb,
            alog_in,
            skip_in,
            bias_in,
            carry_flags,
            token_mask,
        )

    y_local, scan_back = jax.vjp(
        local_scan,
        x_pre,
        bc_pre,
        dt_raw,
        conv_x_w,
        conv_x_b,
        conv_bcw_full,
        conv_bcb_full,
        a_log,
        d_skip,
        dt_bias,
    )
    gated_rows = y_local * jax.nn.silu(gate_pre)
    sq_sum = lax.psum(jnp.sum(gated_rows * gated_rows, axis=1), "tensor")
    inv_g = lax.rsqrt(sq_sum[:, None] / INNER + EPSILON)
    unit_g = gated_rows * inv_g
    hidden = (unit_g * norm_w[None, :] * token_mask[:, None]).astype(jnp.bfloat16)
    branch = lax.psum_scatter(
        dot_nt(hidden, out_full).astype(jnp.bfloat16), "tensor", scatter_dimension=0, tiled=True
    ).astype(jnp.float32)
    output = tokens + branch
    cot_rows = lax.all_gather(cotangent.astype(jnp.bfloat16), "tensor", axis=0, tiled=True)
    z_back, x_back, dt_back, out_back = (z_full, x_full, dt_full, out_full)
    d_hidden = jnp.dot(cot_rows, out_back, preferred_element_type=jnp.float32)
    g_w_out = lax.psum_scatter(dot_tn(cot_rows, hidden), "dp", scatter_dimension=0, tiled=True)
    d_unit = d_hidden * norm_w[None, :] * token_mask[:, None]
    g_norm_w = jnp.sum(d_hidden * unit_g * token_mask[:, None], axis=0)
    inner_sum = lax.psum(jnp.sum(d_unit * unit_g, axis=1), "tensor")
    d_gated = inv_g * (d_unit - unit_g * inner_sum[:, None] / INNER)
    sigmoid_gate = jax.nn.sigmoid(gate_pre)
    d_y = d_gated * gate_pre * sigmoid_gate
    d_gate = d_gated * y_local * sigmoid_gate * (1.0 + gate_pre * (1.0 - sigmoid_gate))
    d_xp, d_bc, d_dt, g_cxw, g_cxb, g_cbw, g_cbb, g_alog, g_skip, g_bias = scan_back(d_y)
    gate_g = d_gate.astype(jnp.bfloat16)
    x_g = d_xp.astype(jnp.bfloat16)
    dt_g = d_dt.astype(jnp.bfloat16)
    bc_g = d_bc.astype(jnp.bfloat16)
    joined = jnp.concatenate([gate_g, x_g, dt_g], axis=1)
    in_grads = lax.psum_scatter(dot_tn(normed, joined), "dp", scatter_dimension=0, tiled=True)
    width_local = w_z.shape[1]
    g_w_z = in_grads[:, :width_local]
    g_w_x = in_grads[:, width_local : 2 * width_local]
    g_w_dt = in_grads[:, 2 * width_local :]
    g_w_bc_part = dot_tn(normed, bc_g)
    summed = dot_nt(gate_g, z_back) + dot_nt(x_g, x_back)
    d_normed = lax.psum_scatter(
        summed + dot_nt(dt_g, dt_back) + dot_nt(bc_g, bc_weight),
        "tensor",
        scatter_dimension=0,
        tiled=True,
    )
    g_gain_part = jnp.sum(d_normed * unit_rows, axis=0)
    d_unit_r = d_normed * gain_full[None, :]
    d_tokens = cotangent + inv_rms * (
        d_unit_r - unit_rows * jnp.mean(d_unit_r * unit_rows, axis=1, keepdims=True)
    )
    g_w_bc, g_gain, g_conv_bcw, g_conv_bcb = (
        lax.psum_scatter(g_w_bc_part, ("dp", "tensor"), scatter_dimension=0, tiled=True),
        lax.psum_scatter(g_gain_part, ("dp", "tensor"), scatter_dimension=0, tiled=True),
        lax.psum_scatter(g_cbw, ("dp", "tensor"), scatter_dimension=0, tiled=True),
        lax.psum_scatter(g_cbb, ("dp", "tensor"), scatter_dimension=0, tiled=True),
    )
    g_cxw, g_cxb, g_alog, g_skip, g_bias, g_norm_w = lax.psum(
        (g_cxw, g_cxb, g_alog, g_skip, g_bias, g_norm_w), "dp"
    )
    return (
        output,
        d_tokens,
        g_gain,
        g_w_z,
        g_w_x,
        g_w_dt,
        g_w_bc,
        g_w_out,
        g_cxw,
        g_cxb,
        g_conv_bcw,
        g_conv_bcb,
        g_alog,
        g_skip,
        g_bias,
        g_norm_w,
    )


def solution(mesh):
    return jax.shard_map(
        per_device,
        mesh=mesh,
        in_specs=(
            P(("dp", "tensor"), None),
            P(("dp", "tensor")),
            P("dp", "tensor"),
            P("dp", "tensor"),
            P("dp", "tensor"),
            P(("dp", "tensor"), None),
            P("dp", "tensor"),
            P("tensor", None),
            P("tensor"),
            P(("dp", "tensor"), None),
            P(("dp", "tensor")),
            P("tensor"),
            P("tensor"),
            P("tensor"),
            P("tensor"),
            P("dp"),
            P("dp"),
            P(("dp", "tensor"), None),
        ),
        out_specs=(
            P(("dp", "tensor"), None),
            P(("dp", "tensor"), None),
            P(("dp", "tensor")),
            P("dp", "tensor"),
            P("dp", "tensor"),
            P("dp", "tensor"),
            P(("dp", "tensor"), None),
            P("dp", "tensor"),
            P("tensor", None),
            P("tensor"),
            P(("dp", "tensor"), None),
            P(("dp", "tensor")),
            P("tensor"),
            P("tensor"),
            P("tensor"),
            P("tensor"),
        ),
        check_vma=False,
    )
```

profile of v0, /device:TPU:0, one launch (start us, length us, event | category | flops | bytes accessed | tf_op | source)
XLA Modules:
  0.0 878.6 jit_solution(2588290233400417949)
XLA Ops:
  10.9 42.0 %all-reduce.35 = (f32[1024]{0:T(1024)S(1)}, f32[256]{0:T(256)}) all-reduce(f32[1024]{0:T(1024)S(1)} %dynamic-update-slice, f32[256]{0:T(256)S(1)} %dynamic-update-slice.1), channel_id=1, replica_groups=mesh['dp'=16,'tensor'=2] {'dp','tensor'}, use_global_device_ids=true, to_apply=%add.29 | all-reduce | flops 1280 | bytes 10240
  60.5 21.4 %all-gather.1 = bf16[16,64,16]{1,2,0:T(8,128)(2,1)S(1)} all-gather(bf16[1,64,16]{1,2,0:T(8,128)(2,1)S(1)} %bitcast.308), channel_id=1, replica_groups=mesh['dp'=16,'tensor'=2] {'dp'}, dimensions={0}, use_global_device_ids=true | all-gather | bytes 34816 | tf_op jit(solution)/shard_map/all_gather | solution.py:138
  82.1 64.5 %all-gather = f32[32,8,4]{1,2,0:T(4,128)S(1)} all-gather(f32[1,8,4]{1,2,0:T(4,128)S(1)} %bitcast.309), channel_id=1, replica_groups=mesh['dp'=16,'tensor'=2] {'dp','tensor'}, dimensions={0}, use_global_device_ids=true | all-gather | bytes 4224 | tf_op jit(solution)/shard_map/all_gather | solution.py:126
  146.7 69.6 %all_gather.34 = bf16[1024,256]{1,0:T(8,128)(2,1)S(1)} all-gather(bf16[32,256]{1,0:T(8,128)(2,1)S(1)} %copy-done.52), channel_id=1, replica_groups=mesh['dp'=16,'tensor'=2] {'dp','tensor'}, dimensions={0}, use_global_device_ids=true | all-gather | bytes 540672 | tf_op jit(solution)/shard_map/all_gather | solution.py:124
  233.0 6.9 fusion.36
  245.6 6.7 fusion.68
  261.3 19.7 %fusion.35 = f32[4,256,16,64]{1,3,2,0:T(8,128)S(1)} fusion(f32[4,256,16,64]{1,3,2,0:T(8,128)S(1)} %bitcast.260, f32[4,256,16,64]{1,0,3,2:T(4,128)S(1)} %copy-done.6, f32[4,256,16]{1,2,0:T(8,128)S(1)} %bitcast.279, f32[4,256,16]{1,2,0:T(8,128)S(1)} %convolution_bitcast_fusion.2, f32[4,256,256]{2,1,0:T(8,128)S(1)} %copy-done.30, ...), kind=kOutput, calls=%fused_computation.44 | convolution fusion | flops 3242196992 | bytes 13893696 | tf_op jit(solution)/shard_map/jvp(sijh,sjhp->sihp)/dot_general | solution.py:68
  286.9 10.0 %multiply_reduce_fusion.10 = (f32[1024]{0:T(1024)S(1)}, f32[1024,1024]{0,1:T(8,128)}, f32[1024,1024]{0,1:T(8,128)}) fusion(f32[1024,1024]{0,1:T(8,128)} %bitcast.255, bf16[1024,1024]{1,0:T(8,128)(2,1)} %all-gather.8.cloned.1.call-done, bf16[1024,1024]{1,0:T(8,128)(2,1)} %all-gather.12.cloned.1.call-done), kind=kOutput, calls=%fused_computation.61 | convolution fusion | flops 2154822656 | bytes 16781312 | tf_op jit(solution)/shard_map/dot_general | solution.py:147
  301.9 9.4 %multiply_reduce_fusion.2 = (f32[1024]{0:T(1024)}, f32[1024]{0:T(1024)S(1)}, f32[1024,1024]{0,1:T(8,128)}) fusion(f32[1024,1024]{0,1:T(8,128)} %get-tuple-element.126, f32[1024]{0:T(1024)S(1)} %fusion.133, f32[1024]{0:T(1024)S(1)} %add_rsqrt_fusion, f32[1024]{0:T(1024)S(1)} %copy-done.69, bf16[1024,1024]{1,0:T(8,128)(2,1)} %all-gather.16.cloned.1.call-done, ...), kind=kOutput, calls=%fused_computation.46 | convolution fusion | flops 2155870208 | bytes 12603392 | tf_op jit(solution)/shard_map/dot_general | solution.py:192
  316.2 11.7 %multiply_reduce_fusion.3 = (f32[1024]{0:T(1024)}, f32[1024,1024]{0,1:T(8,128)}, bf16[1024,1024]{0,1:T(8,128)(2,1)}) fusion(f32[1024,1024]{0,1:T(8,128)} %get-tuple-element.133, f32[1024,1024]{0,1:T(8,128)} %get-tuple-element.165, f32[1024]{0:T(1024)S(1)} %psum.57, f32[1024,1024]{0,1:T(8,128)} %get-tuple-element.126, f32[1024]{0:T(1024)S(1)} %fusion.133, ...), kind=kLoop, calls=%fused_computation.47 | loop fusion | flops 26213376 | bytes 27283456 | tf_op jit(solution)/shard_map/transpose(jvp())/reduce_sum | solution.py:87
  327.8 5.7 reshape.339
  338.6 7.0 fusion.79
  345.6 27.4 %fusion.8 = (f32[4,256,16]{1,2,0:T(8,128)}, f32[4,256,16]{1,2,0:T(8,128)}, f32[4,256,16]{1,2,0:T(8,128)}, f32[4,256,256]{2,1,0:T(8,128)S(1)}) fusion(f32[4,256,16]{1,2,0:T(8,128)S(1)} %bitcast.280, f32[4,256,16]{1,2,0:T(8,128)S(1)} %convolution_bitcast_fusion.2, f32[4,256,256]{2,1,0:T(8,128)S(1)} %copy-done.31, pred[256,256]{1,0:T(8,128)(4,1)S(1)} %copy-done.34, ...), kind=kOutput, calls=%fused_computation.11 | convolution fusion | flops 3275440128 | bytes 10878976 | tf_op jit(solution)/shard_map/transpose(jvp(sijh,sjhp->sihp))/dot_general | solution.py:68
  381.9 6.8 fusion.74
  396.5 15.7 %bitcast_add_fusion = f32[4,256,16,64]{1,3,2,0:T(8,128)S(1)} fusion(f32[4,256,16,64]{1,3,2,0:T(8,128)S(1)} %fusion.62, f32[4,256,16,64]{1,0,3,2:T(4,128)S(1)} %copy-done.9, f32[4,256,16]{1,2,0:T(8,128)S(1)} %bitcast.281, f32[4,256,16]{1,2,0:T(8,128)S(1)} %convolution_bitcast_fusion.2, f32[4,256,256]{2,1,0:T(8,128)S(1)} %copy-done.31, ...), kind=kOutput, calls=%fused_computation.39 | convolution fusion | flops 3242196992 | bytes 13893696 | tf_op jit(solution)/shard_map/transpose(jvp(sijh,sjhp->sihp))/dot_general | solution.py:68
  425.2 6.4 fusion.143
  463.0 7.5 convolution_convert_fusion
  470.8 10.8 %fusion.21 = f32[1024,2064]{1,0:T(8,128)} fusion(bf16[1024,1024]{1,0:T(8,128)(2,1)} %all-gather.8.cloned.1.call-done, bf16[1024,16]{0,1:T(8,128)(2,1)S(1)} %get-tuple-element.117, bf16[1024,1024]{0,1:T(8,128)(2,1)} %copy-done.18, bf16[1024,1024]{0,1:T(8,128)(2,1)S(1)} %copy-done.17), kind=kOutput, calls=%fused_computation.25 | convolution fusion | flops 4341202944 | bytes 14778368 | tf_op jit(solution)/shard_map/dot_general | solution.py:98
  485.1 7.2 convolution_bitcast_fusion
  498.8 57.7 %all-reduce.36 = (f32[1024,4]{0,1:T(4,128)}, f32[1024]{0:T(1024)}, f32[16]{0:T(128)}, f32[16]{0:T(128)}, f32[16]{0:T(128)}, /*index=5*/f32[1024]{0:T(1024)}) all-reduce(f32[1024,4]{0,1:T(4,128)S(1)} %pad_add_fusion.3, f32[1024]{0:T(1024)S(1)} %copy-done.45, ...), channel_id=1, replica_groups=mesh['dp'=16,'tensor'=2] {'dp'}, use_global_device_ids=true, to_apply=%region_26.27 | all-reduce | flops 6192 | bytes 49536 | tf_op jit(solution)/shard_map/psum | solution.py:231
  558.9 38.5 %all-reduce.34 = (f32[1024]{0:T(1024)S(1)}, f32[256,4]{0,1:T(4,128)S(1)}, f32[256]{0:T(256)S(1)}) all-reduce(f32[1024]{0:T(1024)S(1)} %get-tuple-element.86, f32[256,4]{0,1:T(4,128)S(1)} %pad_add_fusion.4, f32[256]{0:T(256)S(1)} %copy-done.71), channel_id=4, replica_groups=mesh['dp'=16,'tensor'=2] {'dp','tensor'}, use_global_device_ids=true, to_apply=%region_18.19.clone | all-reduce | flops 2304 | bytes 18432
  604.4 54.9 %reduce-scatter.13.cloned.1.call-done = f32[64,2064]{1,0:T(8,128)} async-done(((f32[1024,2064]{1,0:T(8,128)}), f32[64,2064]{1,0:T(8,128)}) %reduce-scatter.13.cloned.1.call-update) | async-done | bytes 528400 | tf_op jit(solution)/shard_map/reduce_scatter | solution.py:207
  662.7 135.7 %reduce-scatter.15.cloned.1.call-done = f32[32,256]{1,0:T(8,128)} async-done(((f32[1024,256]{1,0:T(8,128)}), f32[32,256]{1,0:T(8,128)}) %reduce-scatter.15.cloned.1.call-update) | async-done | bytes 32784 | tf_op jit(solution)/shard_map/reduce_scatter | solution.py:226
  798.4 73.2 %reduce-scatter.17.cloned.1.call-done = f32[64,1024]{1,0:T(8,128)} async-done(((f32[1024,1024]{1,0:T(8,128)}), f32[64,1024]{1,0:T(8,128)}) %reduce-scatter.17.cloned.1.call-update) | async-done | bytes 262160
  (317 shorter events, 145.7 us)
Async XLA Ops:
  7.2 210.3 %all-gather.8.cloned.1.call-start = ((), (), s32[]{:S(2)}) async-start(), calls=%async_computation.5 | async-start | bytes 3145728 | tf_op jit(solution)/shard_map/all_gather | solution.py:134
  53.0 93.7 %copy-start.52 = (bf16[32,256]{1,0:T(8,128)(2,1)S(1)}, bf16[32,256]{1,0:T(8,128)(2,1)}, u32[]{:S(2)}) copy-start(bf16[32,256]{1,0:T(8,128)(2,1)} %param.23) | copy-start | bytes 49156
  55.9 161.7 %copy-start.88 = (f32[16]{0:T(128)S(1)}, f32[16]{0:T(128)}, u32[]{:S(2)}) copy-start(f32[16]{0:T(128)} %param.31) | copy-start | bytes 196
  55.9 172.4 %all-gather.10.cloned.1.call-start = ((), (), s32[]{:S(2)}) async-start(), calls=%async_computation.6 | async-start | bytes 2228224 | tf_op jit(solution)/shard_map/all_gather | solution.py:137
  56.6 230.2 %all-gather.12.cloned.1.call-start = ((), (), s32[]{:S(2)}) async-start(), calls=%async_computation.7 | async-start | bytes 2228224 | tf_op jit(solution)/shard_map/all_gather | solution.py:136
  57.4 244.5 %all-gather.16.cloned.1.call-start = ((), (), s32[]{:S(2)}) async-start(), calls=%async_computation.10 | async-start | bytes 3145728 | tf_op jit(solution)/shard_map/all_gather | solution.py:190
  58.6 243.2 %all-gather.14.cloned.1.call-start = ((), (), s32[]{:S(2)}) async-start(), calls=%async_computation.8 | async-start | bytes 2228224 | tf_op jit(solution)/shard_map/all_gather | solution.py:139
  59.2 497.3 %reduce-scatter.11.cloned.1.call-start = ((), (), s32[]{:S(2)}) async-start(), calls=%async_computation.11 | async-start | bytes 6291456 | tf_op jit(solution)/shard_map/reduce_scatter | solution.py:214
  60.1 199.3 %copy-start.33 = (pred[256,256]{1,0:T(8,128)(4,1)}, pred[256,256]{1,0:T(8,128)(4,1)S(1)}, u32[]{:S(2)}) copy-start(pred[256,256]{1,0:T(8,128)(4,1)S(1)} %convert_compare_fusion) | copy-start | bytes 196612
  60.1 160.3 %copy-start.84 = (f32[16]{0:T(128)}, f32[16]{0:T(128)S(1)}, u32[]{:S(2)}) copy-start(f32[16]{0:T(128)S(1)} %exponential_negate_fusion) | copy-start | bytes 196
  146.7 78.1 %copy-start.57 = (f32[256,1]{0,1:T(1,128)}, f32[256,1]{0,1:T(1,128)S(1)}, u32[]{:S(2)}) copy-start(f32[256,1]{0,1:T(1,128)S(1)} %get-tuple-element.157) | copy-start | bytes 3076
  146.7 78.1 %copy-start.58 = (f32[256,1]{0,1:T(1,128)}, f32[256,1]{0,1:T(1,128)S(1)}, u32[]{:S(2)}) copy-start(f32[256,1]{0,1:T(1,128)S(1)} %get-tuple-element.158) | copy-start | bytes 3076
  146.7 78.1 %copy-start.60 = (f32[256,1]{0,1:T(1,128)}, f32[256,1]{0,1:T(1,128)S(1)}, u32[]{:S(2)}) copy-start(f32[256,1]{0,1:T(1,128)S(1)} %get-tuple-element.159) | copy-start | bytes 3076
  146.7 78.1 %copy-start.62 = (f32[256,1]{0,1:T(1,128)}, f32[256,1]{0,1:T(1,128)S(1)}, u32[]{:S(2)}) copy-start(f32[256,1]{0,1:T(1,128)S(1)} %get-tuple-element.156) | copy-start | bytes 3076
  462.3 136.9 %reduce-scatter.9.cloned.1.call-start = ((), (), s32[]{:S(2)}) async-start(), calls=%async_computation.9 | async-start | bytes 3145728 | tf_op jit(solution)/shard_map/reduce_scatter | solution.py:186
  470.6 188.8 %reduce-scatter.13.cloned.1.call-start = ((), (), s32[]{:S(2)}) async-start(), calls=%async_computation.12 | async-start | bytes 9469952 | tf_op jit(solution)/shard_map/reduce_scatter | solution.py:207
  481.6 316.8 %reduce-scatter.15.cloned.1.call-start = ((), (), s32[]{:S(2)}) async-start(), calls=%async_computation.13 | async-start | bytes 1081344 | tf_op jit(solution)/shard_map/reduce_scatter | solution.py:226
  485.1 386.4 %reduce-scatter.17.cloned.1.call-start = ((), (), s32[]{:S(2)}) async-start(), calls=%async_computation.14 | async-start | bytes 4456448
  497.8 58.6 %copy-start.72 = (f32[256]{0:T(256)S(1)}, f32[256]{0:T(256)}, u32[]{:S(2)}) copy-start(f32[256]{0:T(256)} %get-tuple-element.97) | copy-start | bytes 3076
  497.9 58.6 %copy-start.10 = (f32[512,1024]{1,0:T(8,128)S(1)}, f32[512,1024]{1,0:T(8,128)}, u32[]{:S(2)}) copy-start(f32[512,1024]{1,0:T(8,128)} %param.18) | copy-start | bytes 6291460
  497.9 58.6 %copy-start.39 = (f32[1024]{0:T(1024)S(1)}, f32[1024]{0:T(1024)}, u32[]{:S(2)}) copy-start(f32[1024]{0:T(1024)} %copy-done.38) | copy-start | bytes 12292
  497.9 58.6 %copy-start.41 = (f32[512]{0:T(512)S(1)}, f32[512]{0:T(512)}, u32[]{:S(2)}) copy-start(f32[512]{0:T(512)} %copy-done.40) | copy-start | bytes 6148
  497.9 61.0 %copy-start.71 = (f32[256]{0:T(256)S(1)}, f32[256]{0:T(256)}, u32[]{:S(2)}) copy-start(f32[256]{0:T(256)} %get-tuple-element.96) | copy-start | bytes 3076
  599.2 272.3 %copy-start.1 = (s32[4]{0:T(128)S(1)}, s32[4]{0:T(128)}, u32[]{:S(2)}) copy-start(s32[4]{0:T(128)} %param.34) | copy-start | bytes 52
  (83 other events, 690.5 us)
Sparse Core Ops, SparseCore 0:
  56.0 33.3 all-gather.7
  91.5 41.5 all-gather.9
  135.3 40.3 all-gather.11
  177.1 35.8 all-gather.15
  215.0 41.4 all-gather.13
  462.4 50.2 reduce-scatter.10
  515.6 31.8 reduce-scatter.8
  551.6 107.7 reduce-scatter.12
  662.2 136.1 reduce-scatter.14
  802.6 68.8 reduce-scatter.16
where the time goes:
time: 882 us; the launch traced here: 879 us
  blocking collectives  304 us (34%)
  waiting for transfers between devices  266 us (30%)
  matrix products  167 us (19%)
  other arithmetic  79 us (9%)
  local copies, waits for them, and re-layouts  46.7 us (5%)
  between operations  16.3 us (2%)
    reduce_scatter x1, waiting for transfers between devices, per_device(): lax.psum_scatter(g_w_bc_part, ('dp', 'tensor'), scatter_dimension=0, tile...  136 us
    unnamed x2, blocking collectives  80.5 us
    unnamed x11, waiting for transfers between devices  75.2 us
    all_gather x1, blocking collectives, per_device(): lax.all_gather(w_bc.astype(jnp.float32), ('dp', 'tensor'), axis=0, tiled=...  69.6 us
    all_gather x1, blocking collectives, per_device(): lax.all_gather(conv_bc_w, ('dp', 'tensor'), axis=0, tiled=True)  64.5 us
    dot_general x3, matrix products, scan_heads(): jnp.einsum('sijh,sjhp->sihp', mixing, inputs, precision=HIGHEST_PREC)  62.8 us
    psum x1, blocking collectives, per_device(): lax.psum((g_cxw, g_cxb, g_alog, g_skip, g_bias, g_norm_w), 'dp')  57.7 us
    reduce_scatter x1, waiting for transfers between devices, per_device(): lax.psum_scatter(dot_tn(normed, joined), 'dp', scatter_dimension=0, tiled...  54.9 us
  transfers between devices with their start and end apart: 10, of which 3 were waited for; matrix products, arithmetic and copies ran while one was open for 14% of the time, Pallas kernels for 0%

commit v1 on v0

--- a/solution.py
+++ b/solution.py
@@ -9,6 +9,27 @@
 BLOCK = 256
 EPSILON = 1e-05
 HIGHEST_PREC = lax.Precision.HIGHEST
+
+
+def in_order(parts, dim):
+    parts = jnp.moveaxis(parts, 0, dim)
+    lengths = parts.shape
+    return parts.reshape(*lengths[:dim], lengths[dim] * lengths[dim + 1], *lengths[dim + 2 :])
+
+
+def collected_by_bits(x, axis):
+    peers, here = (lax.axis_size(axis), lax.axis_index(axis))
+    blocks, apart = (x[None], 1)
+    while apart < peers:
+        theirs = lax.ppermute(blocks, axis, [(i, i ^ apart) for i in range(peers)])
+        low = here & apart == 0
+        blocks = jnp.concatenate([jnp.where(low, blocks, theirs), jnp.where(low, theirs, blocks)])
+        apart *= 2
+    return blocks
+
+
+def collect(x, axis, dim):
+    return in_order(collected_by_bits(x, axis), dim)
 
 
 def shift_rows(values, lag_rows):
@@ -123,7 +144,7 @@
     bc_full, gain_full, conv_bcw_full, conv_bcb_full = (
         lax.all_gather(w_bc.astype(jnp.float32), ("dp", "tensor"), axis=0, tiled=True),
         lax.all_gather(norm_gain, ("dp", "tensor"), axis=0, tiled=True),
-        lax.all_gather(conv_bc_w, ("dp", "tensor"), axis=0, tiled=True),
+        collect(conv_bc_w, ("dp", "tensor"), 0),
         lax.all_gather(conv_bc_b, ("dp", "tensor"), axis=0, tiled=True),
     )
     bc_weight = bc_full.astype(jnp.bfloat16)

time: 882 us -> 841 us (0.954)
  blocking collectives: 304 us -> 237 us
  waiting for transfers between devices: 266 us -> 288 us
    all_gather x1 -> x0, blocking collectives: 64.5 us -> none  [per_device(): lax.all_gather(conv_bc_w, ('dp', 'tensor'), axis=0, tiled=True)]
    all_gather x1, waiting for transfers between devices: 0.02 us -> 12.2 us  [per_device(): lax.all_gather(w_out, 'dp', axis=0, tiled=True)]
    unnamed x211 -> x210, local copies, waits for them, and re-layouts: 23.9 us -> 24.1 us
  transfers between devices with their start and end apart: 10 -> 15, of which waited for: 3 -> 7; matrix products, arithmetic and copies ran while one was open for 14% -> 15% of each run, Pallas kernels for 0% -> 0%
where the time goes in v1:
time: 841 us; the launch traced here: 837 us
  waiting for transfers between devices  288 us (34%)
  blocking collectives  237 us (28%)
  matrix products  166 us (20%)
  other arithmetic  79.5 us (9%)
  local copies, waits for them, and re-layouts  47.1 us (6%)
  between operations  16.4 us (2%)
    reduce_scatter x1, waiting for transfers between devices, per_device(): lax.psum_scatter(g_w_bc_part, ('dp', 'tensor'), scatter_dimension=0, tile...  136 us
    unnamed x2, blocking collectives  79.6 us
    unnamed x11, waiting for transfers between devices  74.4 us
    all_gather x1, blocking collectives, per_device(): lax.all_gather(w_bc.astype(jnp.float32), ('dp', 'tensor'), axis=0, tiled=...  69.1 us
    dot_general x3, matrix products, scan_heads(): jnp.einsum('sijh,sjhp->sihp', mixing, inputs, precision=HIGHEST_PREC)  62.9 us
    psum x1, blocking collectives, per_device(): lax.psum((g_cxw, g_cxb, g_alog, g_skip, g_bias, g_norm_w), 'dp')  58.7 us
    reduce_scatter x1, waiting for transfers between devices, per_device(): lax.psum_scatter(dot_tn(normed, joined), 'dp', scatter_dimension=0, tiled...  58.2 us
    unnamed x210, local copies, waits for them, and re-layouts  24.1 us
  transfers between devices with their start and end apart: 15, of which 7 were waited for; matrix products, arithmetic and copies ran while one was open for 15% of the time, Pallas kernels for 0%

profile of v1, /device:TPU:0, one launch (start us, length us, event | category | flops | bytes accessed | tf_op | source)
XLA Modules:
  0.0 837.1 jit_solution(13545724482724138806)
XLA Ops:
  10.9 42.0 %all-reduce.35 = (f32[1024]{0:T(1024)S(1)}, f32[256]{0:T(256)}) all-reduce(f32[1024]{0:T(1024)S(1)} %dynamic-update-slice, f32[256]{0:T(256)S(1)} %dynamic-update-slice.1), channel_id=1, replica_groups=mesh['dp'=16,'tensor'=2] {'dp','tensor'}, use_global_device_ids=true, to_apply=%add.29 | all-reduce | flops 1280 | bytes 10240
  61.4 69.1 %all_gather.31 = bf16[1024,256]{1,0:T(8,128)(2,1)S(1)} all-gather(bf16[32,256]{1,0:T(8,128)(2,1)S(1)} %copy-done.52), channel_id=1, replica_groups=mesh['dp'=16,'tensor'=2] {'dp','tensor'}, dimensions={0}, use_global_device_ids=true | all-gather | bytes 540672 | tf_op jit(solution)/shard_map/all_gather | solution.py:145
  139.5 19.4 %all-gather = bf16[16,64,16]{1,2,0:T(8,128)(2,1)S(1)} all-gather(bf16[1,64,16]{1,2,0:T(8,128)(2,1)S(1)} %bitcast.310), channel_id=1, replica_groups=mesh['dp'=16,'tensor'=2] {'dp'}, dimensions={0}, use_global_device_ids=true | all-gather | bytes 34816 | tf_op jit(solution)/shard_map/all_gather | solution.py:159
  176.0 6.9 fusion.36
  188.5 6.8 fusion.68
  204.4 19.7 %fusion.35 = f32[4,256,16,64]{1,3,2,0:T(8,128)S(1)} fusion(f32[4,256,16,64]{1,3,2,0:T(8,128)S(1)} %bitcast.262, f32[4,256,16,64]{1,0,3,2:T(4,128)S(1)} %copy-done.6, f32[4,256,16]{1,2,0:T(8,128)S(1)} %bitcast.281, f32[4,256,16]{1,2,0:T(8,128)S(1)} %convolution_bitcast_fusion.2, f32[4,256,256]{2,1,0:T(8,128)S(1)} %copy-done.30, ...), kind=kOutput, calls=%fused_computation.44 | convolution fusion | flops 3242196992 | bytes 13893696 | tf_op jit(solution)/shard_map/jvp(sijh,sjhp->sihp)/dot_general | solution.py:89
  230.0 10.2 %multiply_reduce_fusion.10 = (f32[1024]{0:T(1024)S(1)}, f32[1024,1024]{0,1:T(8,128)}, f32[1024,1024]{0,1:T(8,128)}) fusion(f32[1024,1024]{0,1:T(8,128)} %bitcast.257, bf16[1024,1024]{1,0:T(8,128)(2,1)} %all-gather.7.cloned.1.call-done, bf16[1024,1024]{1,0:T(8,128)(2,1)} %all-gather.11.cloned.1.call-done), kind=kOutput, calls=%fused_computation.61 | convolution fusion | flops 2154822656 | bytes 16781312 | tf_op jit(solution)/shard_map/dot_general | solution.py:168
  245.1 12.2 %all-gather.13.cloned.1.call-done = bf16[1024,1024]{1,0:T(8,128)(2,1)} async-done(((bf16[64,1024]{1,0:T(8,128)(2,1)}), bf16[1024,1024]{1,0:T(8,128)(2,1)}) %all-gather.13.cloned.1.call-update) | async-done | bytes 2097168 | tf_op jit(solution)/shard_map/all_gather | solution.py:160
  257.3 9.4 %multiply_reduce_fusion.2 = (f32[1024]{0:T(1024)}, f32[1024]{0:T(1024)S(1)}, f32[1024,1024]{0,1:T(8,128)}) fusion(f32[1024,1024]{0,1:T(8,128)} %get-tuple-element.126, f32[1024]{0:T(1024)S(1)} %fusion.133, f32[1024]{0:T(1024)S(1)} %add_rsqrt_fusion, f32[1024]{0:T(1024)S(1)} %copy-done.69, bf16[1024,1024]{1,0:T(8,128)(2,1)} %all-gather.15.cloned.1.call-done, ...), kind=kOutput, calls=%fused_computation.46 | convolution fusion | flops 2155870208 | bytes 12603392 | tf_op jit(solution)/shard_map/dot_general | solution.py:213
  271.6 11.7 %multiply_reduce_fusion.3 = (f32[1024]{0:T(1024)}, f32[1024,1024]{0,1:T(8,128)}, bf16[1024,1024]{0,1:T(8,128)(2,1)}) fusion(f32[1024,1024]{0,1:T(8,128)} %get-tuple-element.133, f32[1024,1024]{0,1:T(8,128)} %get-tuple-element.175, f32[1024]{0:T(1024)S(1)} %psum.57, f32[1024,1024]{0,1:T(8,128)} %get-tuple-element.126, f32[1024]{0:T(1024)S(1)} %fusion.133, ...), kind=kLoop, calls=%fused_computation.47 | loop fusion | flops 26213376 | bytes 27283456 | tf_op jit(solution)/shard_map/transpose(jvp())/reduce_sum | solution.py:108
  283.3 5.7 reshape.343
  294.1 7.0 fusion.79
  301.1 27.4 %fusion.8 = (f32[4,256,16]{1,2,0:T(8,128)}, f32[4,256,16]{1,2,0:T(8,128)}, f32[4,256,16]{1,2,0:T(8,128)}, f32[4,256,256]{2,1,0:T(8,128)S(1)}) fusion(f32[4,256,16]{1,2,0:T(8,128)S(1)} %bitcast.282, f32[4,256,16]{1,2,0:T(8,128)S(1)} %convolution_bitcast_fusion.2, f32[4,256,256]{2,1,0:T(8,128)S(1)} %copy-done.31, pred[256,256]{1,0:T(8,128)(4,1)S(1)} %copy-done.34, ...), kind=kOutput, calls=%fused_computation.11 | convolution fusion | flops 3275440128 | bytes 10878976 | tf_op jit(solution)/shard_map/transpose(jvp(sijh,sjhp->sihp))/dot_general | solution.py:89
  337.3 6.8 fusion.74
  351.9 15.7 %bitcast_add_fusion = f32[4,256,16,64]{1,3,2,0:T(8,128)S(1)} fusion(f32[4,256,16,64]{1,3,2,0:T(8,128)S(1)} %fusion.62, f32[4,256,16,64]{1,0,3,2:T(4,128)S(1)} %copy-done.9, f32[4,256,16]{1,2,0:T(8,128)S(1)} %bitcast.283, f32[4,256,16]{1,2,0:T(8,128)S(1)} %convolution_bitcast_fusion.2, f32[4,256,256]{2,1,0:T(8,128)S(1)} %copy-done.31, ...), kind=kOutput, calls=%fused_computation.39 | convolution fusion | flops 3242196992 | bytes 13893696 | tf_op jit(solution)/shard_map/transpose(jvp(sijh,sjhp->sihp))/dot_general | solution.py:89
  380.6 6.4 fusion.143
  418.5 6.8 convolution_convert_fusion
  425.6 10.8 %fusion.21 = f32[1024,2064]{1,0:T(8,128)} fusion(bf16[1024,1024]{1,0:T(8,128)(2,1)} %all-gather.7.cloned.1.call-done, bf16[1024,16]{0,1:T(8,128)(2,1)S(1)} %get-tuple-element.117, bf16[1024,1024]{0,1:T(8,128)(2,1)} %copy-done.18, bf16[1024,1024]{0,1:T(8,128)(2,1)S(1)} %copy-done.17), kind=kOutput, calls=%fused_computation.25 | convolution fusion | flops 4341202944 | bytes 14778368 | tf_op jit(solution)/shard_map/dot_general | solution.py:119
  440.1 7.3 convolution_bitcast_fusion
  453.9 58.7 %all-reduce.36 = (f32[1024,4]{0,1:T(4,128)}, f32[1024]{0:T(1024)}, f32[16]{0:T(128)}, f32[16]{0:T(128)}, f32[16]{0:T(128)}, /*index=5*/f32[1024]{0:T(1024)}) all-reduce(f32[1024,4]{0,1:T(4,128)S(1)} %pad_add_fusion.3, f32[1024]{0:T(1024)S(1)} %copy-done.45, ...), channel_id=1, replica_groups=mesh['dp'=16,'tensor'=2] {'dp'}, use_global_device_ids=true, to_apply=%region_26.27 | all-reduce | flops 6192 | bytes 49536 | tf_op jit(solution)/shard_map/psum | solution.py:252
  514.9 37.6 %all-reduce.34 = (f32[1024]{0:T(1024)S(1)}, f32[256,4]{0,1:T(4,128)S(1)}, f32[256]{0:T(256)S(1)}) all-reduce(f32[1024]{0:T(1024)S(1)} %get-tuple-element.86, f32[256,4]{0,1:T(4,128)S(1)} %pad_add_fusion.4, f32[256]{0:T(256)S(1)} %copy-done.71), channel_id=4, replica_groups=mesh['dp'=16,'tensor'=2] {'dp','tensor'}, use_global_device_ids=true, to_apply=%region_18.19.clone | all-reduce | flops 2304 | bytes 18432
  559.6 58.2 %reduce-scatter.13.cloned.1.call-done = f32[64,2064]{1,0:T(8,128)} async-done(((f32[1024,2064]{1,0:T(8,128)}), f32[64,2064]{1,0:T(8,128)}) %reduce-scatter.13.cloned.1.call-update) | async-done | bytes 528400 | tf_op jit(solution)/shard_map/reduce_scatter | solution.py:228
  621.0 136.1 %reduce-scatter.15.cloned.1.call-done = f32[32,256]{1,0:T(8,128)} async-done(((f32[1024,256]{1,0:T(8,128)}), f32[32,256]{1,0:T(8,128)}) %reduce-scatter.15.cloned.1.call-update) | async-done | bytes 32784 | tf_op jit(solution)/shard_map/reduce_scatter | solution.py:247
  757.1 72.9 %reduce-scatter.17.cloned.1.call-done = f32[64,1024]{1,0:T(8,128)} async-done(((f32[1024,1024]{1,0:T(8,128)}), f32[64,1024]{1,0:T(8,128)}) %reduce-scatter.17.cloned.1.call-update) | async-done | bytes 262160
  (336 shorter events, 155.9 us)
Async XLA Ops:
  7.2 153.5 %all-gather.7.cloned.1.call-start = ((), (), s32[]{:S(2)}) async-start(), calls=%async_computation.5 | async-start | bytes 3145728 | tf_op jit(solution)/shard_map/all_gather | solution.py:155
  53.0 77.7 %copy-start.95 = (f32[16]{0:T(128)S(1)}, f32[16]{0:T(128)}, u32[]{:S(2)}) copy-start(f32[16]{0:T(128)} %param.29) | copy-start | bytes 196
  53.0 86.5 %copy-start.76 = (bf16[64,16]{0,1:T(8,128)(2,1)S(1)}, bf16[64,16]{0,1:T(8,128)(2,1)}, u32[]{:S(2)}) copy-start(bf16[64,16]{0,1:T(8,128)(2,1)} %param.22) | copy-start | bytes 6148
  55.9 104.8 %copy-start.88 = (f32[16]{0:T(128)S(1)}, f32[16]{0:T(128)}, u32[]{:S(2)}) copy-start(f32[16]{0:T(128)} %param.31) | copy-start | bytes 196
  55.9 115.4 %all-gather.9.cloned.1.call-start = ((), (), s32[]{:S(2)}) async-start(), calls=%async_computation.6 | async-start | bytes 2228224 | tf_op jit(solution)/shard_map/all_gather | solution.py:158
  56.6 173.3 %all-gather.11.cloned.1.call-start = ((), (), s32[]{:S(2)}) async-start(), calls=%async_computation.7 | async-start | bytes 2228224 | tf_op jit(solution)/shard_map/all_gather | solution.py:157
  57.4 187.7 %all-gather.15.cloned.1.call-start = ((), (), s32[]{:S(2)}) async-start(), calls=%async_computation.10 | async-start | bytes 3145728 | tf_op jit(solution)/shard_map/all_gather | solution.py:211
  58.6 198.7 %all-gather.13.cloned.1.call-start = ((), (), s32[]{:S(2)}) async-start(), calls=%async_computation.8 | async-start | bytes 2228224 | tf_op jit(solution)/shard_map/all_gather | solution.py:160
  58.7 71.9 %collective-permute-start = (f32[1,8,4]{1,2,0:T(4,128)S(1)}, f32[1,8,4]{1,2,0:T(4,128)S(1)}, u32[]{:S(2)}, u32[]{:S(2)}) collective-permute-start(f32[1,8,4]{1,2,0:T(4,128)S(1)} %bitcast.311), channel_id=1, source_target_pairs={{0,1},{1,0},{2,3},{3,2},{4,5},{5,4},{6,7},{7,6},{8,9},{9,8},{10,11... | collective-permute-start | bytes 392 | tf_op jit(solution)/shard_map/ppermute | solution.py:24
  61.0 451.6 %reduce-scatter.11.cloned.1.call-start = ((), (), s32[]{:S(2)}) async-start(), calls=%async_computation.11 | async-start | bytes 6291456 | tf_op jit(solution)/shard_map/reduce_scatter | solution.py:235
  130.6 1.2 collective-permute-start.1
  131.8 3.7 collective-permute-start.2
  135.6 3.8 collective-permute-start.3
  139.4 21.0 %collective-permute-start.4 = (f32[16,8,4]{1,2,0:T(4,128)S(1)}, f32[16,8,4]{1,2,0:T(4,128)S(1)}, u32[]{:S(2)}, u32[]{:S(2)}) collective-permute-start(f32[16,8,4]{1,2,0:T(4,128)S(1)} %pad_maximum_fusion.2), channel_id=1, source_target_pairs={{0,16},{1,17},{2,18},{3,19},{4,20},{5,21},{6,22},{7,23},{8,24},{9,... | collective-permute-start | bytes 6152 | tf_op jit(solution)/shard_map/ppermute | solution.py:24
  417.9 136.5 %reduce-scatter.9.cloned.1.call-start = ((), (), s32[]{:S(2)}) async-start(), calls=%async_computation.9 | async-start | bytes 3145728 | tf_op jit(solution)/shard_map/reduce_scatter | solution.py:207
  425.4 192.3 %reduce-scatter.13.cloned.1.call-start = ((), (), s32[]{:S(2)}) async-start(), calls=%async_computation.12 | async-start | bytes 9469952 | tf_op jit(solution)/shard_map/reduce_scatter | solution.py:228
  436.5 320.6 %reduce-scatter.15.cloned.1.call-start = ((), (), s32[]{:S(2)}) async-start(), calls=%async_computation.13 | async-start | bytes 1081344 | tf_op jit(solution)/shard_map/reduce_scatter | solution.py:247
  440.1 390.0 %reduce-scatter.17.cloned.1.call-start = ((), (), s32[]{:S(2)}) async-start(), calls=%async_computation.14 | async-start | bytes 4456448
  453.0 59.6 %copy-start.72 = (f32[256]{0:T(256)S(1)}, f32[256]{0:T(256)}, u32[]{:S(2)}) copy-start(f32[256]{0:T(256)} %get-tuple-element.97) | copy-start | bytes 3076
  453.0 59.6 %copy-start.10 = (f32[512,1024]{1,0:T(8,128)S(1)}, f32[512,1024]{1,0:T(8,128)}, u32[]{:S(2)}) copy-start(f32[512,1024]{1,0:T(8,128)} %param.18) | copy-start | bytes 6291460
  453.0 59.6 %copy-start.39 = (f32[1024]{0:T(1024)S(1)}, f32[1024]{0:T(1024)}, u32[]{:S(2)}) copy-start(f32[1024]{0:T(1024)} %copy-done.38) | copy-start | bytes 12292
  453.0 59.6 %copy-start.41 = (f32[512]{0:T(512)S(1)}, f32[512]{0:T(512)}, u32[]{:S(2)}) copy-start(f32[512]{0:T(512)} %copy-done.40) | copy-start | bytes 6148
  453.0 61.9 %copy-start.71 = (f32[256]{0:T(256)S(1)}, f32[256]{0:T(256)}, u32[]{:S(2)}) copy-start(f32[256]{0:T(256)} %get-tuple-element.96) | copy-start | bytes 3076
  554.3 275.7 %copy-start.1 = (s32[4]{0:T(128)S(1)}, s32[4]{0:T(128)}, u32[]{:S(2)}) copy-start(s32[4]{0:T(128)} %param.34) | copy-start | bytes 52
  (88 other events, 860.9 us)
Sparse Core Ops, SparseCore 0:
  56.0 37.7 all-gather.6
  95.9 42.1 all-gather.8
  140.3 40.3 all-gather.10
  182.1 31.6 all-gather.14
  215.8 41.4 all-gather.12
  418.0 53.0 reduce-scatter.10
  473.9 31.8 reduce-scatter.8
  510.0 107.7 reduce-scatter.12
  620.5 136.5 reduce-scatter.14
  761.4 68.6 reduce-scatter.16
